TPU v7x, 32 devices: a whole 2x2x4 slice. The times are simulated.
32 devices in a mesh: gx: 8 (over z, y), gy: 4 (over x, core).
Axes of the slice: x: 2, y: 2, z: 4, core: 2. Of those that a mesh axis runs over, the one named last changes fastest.
Arguments:
- right_side: float32 [64, 128, 128], P('gy', 'gx'), may hold values from -6 to 9
- diagonal: float32 [64, 128, 128], P('gy', 'gx'), may hold values from 0.02 to 0.5
- horizontal: float32 [64, 128, 128], P('gy', 'gx'), may hold values from 0.1 to 1
- vertical: float32 [128], replicated, may hold values from 0.2 to 2
- precond: float32 [2, 128, 128], replicated, may hold values from -4 to 4
- edge_rows: int32 [2, 64], replicated, may hold values from 0 to 63, as said below
Outputs:
- solution_field: float32 [64, 128, 128], P('gy', 'gx')
- residual: float32 [64, 128, 128], P('gy', 'gx')
- residual_sq: float32 [3], replicated
Inputs may be any that keep to these rules, and one draw needn't show every extreme that they name: Each row of edge_rows lists every number 0 to 63 exactly once.
All inputs are finite; a program needn't handle non-finite values.
Results may differ from a plain program's by a relative error of at most 0.00014.
Values sent between devices are 32-bit elements; how exact they have to be, the bound alone decides.
No kernel may reach another device: no remote copies, remote signals or barrier semaphores. Data moves between devices by JAX's collectives and lax.ppermute only.
A program may use at most 64 MiB of HBM per device.

v0:
```python
import jax
import jax.numpy as jnp
from jax import lax
from jax.sharding import PartitionSpec as P

ITERS = 3


def padded(x, sides, width, wrap):
    for axis, dim in sides:
        devices, length = (lax.axis_size(axis), x.shape[dim])
        up = [(i, (i + 1) % devices) for i in range(devices if wrap else devices - 1)]
        down = [(j, i) for i, j in up]
        last = lax.slice_in_dim(x, length - width, length, axis=dim)
        initial = lax.slice_in_dim(x, 0, width, axis=dim)
        before = lax.ppermute(last, axis, up)
        after = lax.ppermute(initial, axis, down)
        x = jnp.concatenate([before, x, after], axis=dim)
    return x


def local_product(left, right):
    return jnp.sum(left * right)


def on_device(right_side, diagonal, horizontal, vertical, precond, edge_rows):
    rows, cols, levels = right_side.shape
    n_gx = lax.axis_size("gx")
    n_gy = lax.axis_size("gy")
    col_index = lax.axis_index("gx")
    row_index = lax.axis_index("gy")
    total_cells = float(rows * cols * levels * n_gx * n_gy)
    half = n_gx // 2
    panel = (col_index >= half).astype(jnp.int32)
    matrix = lax.dynamic_index_in_dim(precond, panel, 0, keepdims=False)
    east_table = jnp.where(col_index == half - 1, edge_rows[0], edge_rows[1])
    west_table = jnp.where(col_index == half, edge_rows[0], edge_rows[1])
    first_row = row_index * rows
    east_local = lax.dynamic_slice_in_dim(east_table, first_row, rows)
    west_local = lax.dynamic_slice_in_dim(west_table, first_row, rows)
    east_border = (col_index == half - 1) | (col_index == n_gx - 1)
    west_border = (col_index == half) | (col_index == 0)
    solution_field = jnp.zeros_like(right_side)
    residual = right_side
    directions = []
    images = []
    norms = []
    for step in range(ITERS):
        pre = jnp.einsum("yxl,kl->yxk", residual, matrix, precision=lax.Precision.HIGHEST)
        wide = padded(pre, (("gx", 1),), 1, True)
        edges = jnp.stack([wide[:, 0], wide[:, -1]], 0)
        whole = lax.all_gather(edges, "gy", axis=1, tiled=True)
        west_fix = jnp.take(whole[0], west_local, axis=0)
        east_fix = jnp.take(whole[1], east_local, axis=0)
        west = jnp.where(west_border, west_fix, edges[0])
        east = jnp.where(east_border, east_fix, edges[1])
        tall = padded(pre, (("gy", 0),), 1, False)
        flat = jnp.pad(pre, ((0, 0), (0, 0), (1, 1)))
        east_side = jnp.concatenate([pre[:, 1:], east[:, None]], 1)
        west_side = jnp.concatenate([west[:, None], pre[:, :-1]], 1)
        beside = east_side + west_side + tall[2:] + tall[:-2]
        column = flat[:, :, 2:] + flat[:, :, :-2]
        image = diagonal * pre + horizontal * (4.0 * pre - beside) + vertical * (2.0 * pre - column)
        count = len(images)
        terms = [local_product(image, older) for older in images]
        terms = terms + [local_product(residual, older) for older in images]
        terms = terms + [local_product(image, image), local_product(residual, image)]
        if step > 0:
            terms.append(local_product(residual, residual))
        totals = lax.psum(jnp.stack(terms), ("gx", "gy")) / total_cells
        coeffs = totals[:count]
        against = totals[count : 2 * count]
        square = totals[2 * count] - jnp.sum(coeffs * coeffs)
        along = totals[2 * count + 1] - jnp.sum(coeffs * against)
        if step > 0:
            norms.append(totals[2 * count + 2])
        for number in range(count):
            pre = pre - coeffs[number] * directions[number]
            image = image - coeffs[number] * images[number]
        scale = 1.0 / jnp.sqrt(square)
        alpha = along * scale
        direction = pre * scale
        image = image * scale
        solution_field = solution_field + alpha * direction
        residual = residual - alpha * image
        directions.append(direction)
        images.append(image)
    norms.append(lax.psum(local_product(residual, residual), ("gx", "gy")) / total_cells)
    return (solution_field, residual, jnp.stack(norms))


def solution(mesh):
    in_specs = (P("gy", "gx", None), P("gy", "gx", None), P("gy", "gx", None), P(), P(), P())
    out_specs = (P("gy", "gx", None), P("gy", "gx", None), P())
    return jax.shard_map(
        on_device, mesh=mesh, in_specs=in_specs, out_specs=out_specs, check_vma=False
    )
```

profile of v0, /device:TPU:0, one launch (start us, length us, event | category | flops | bytes accessed | tf_op | source)
XLA Modules:
  0.0 243.0 jit_solution(2497374235617542815)
XLA Ops:
  0.7 0.9 copy-done
  1.5 1.2 convolution_bitcast_fusion
  2.7 1.3 collective-permute-start.2
  4.0 3.0 %collective-permute-start.3 = (f32[1,16,128]{2,1,0:T(8,128)S(1)}, f32[1,16,128]{2,1,0:T(8,128)S(1)}, u32[]{:S(2)}, u32[]{:S(2)}) collective-permute-start(f32[1,16,128]{2,1,0:T(8,128)S(1)} %get-tuple-element.48), channel_id=1, source_target_pairs={{0,1},{1,2},{2,3},{4,5},{5,6},{6,7},{8,9},{9,10},{10,11},{12,13},{... | collective-permute-start | bytes 24584 | tf_op jit(solution)/shard_map/ppermute | solution.py:16
  7.1 3.0 %collective-permute-start = (f32[16,1,128]{2,0,1:T(8,128)S(1)}, f32[16,1,128]{2,0,1:T(8,128)S(1)}, u32[]{:S(2)}, u32[]{:S(2)}) collective-permute-start(f32[16,1,128]{2,0,1:T(8,128)S(1)} %bitcast.112), channel_id=1, source_target_pairs={{0,4},{4,8},{8,12},{12,16},{16,20},{20,24},{24,28},{28,0},{1,5},{5... | collective-permute-start | bytes 24584 | tf_op jit(solution)/shard_map/ppermute | solution.py:16
  10.1 3.1 %collective-permute-start.1 = (f32[16,1,128]{2,0,1:T(8,128)S(1)}, f32[16,1,128]{2,0,1:T(8,128)S(1)}, u32[]{:S(2)}, u32[]{:S(2)}) collective-permute-start(f32[16,1,128]{2,0,1:T(8,128)S(1)} %bitcast.111), channel_id=1, source_target_pairs={{4,0},{8,4},{12,8},{16,12},{20,16},{24,20},{28,24},{0,28},{5,1},{9... | collective-permute-start | bytes 24584 | tf_op jit(solution)/shard_map/ppermute | solution.py:17
  13.3 0.7 copy-done.5
  14.8 5.4 %all_gather.9 = f32[2,64,128]{2,1,0:T(8,128)S(1)} all-gather(f32[2,16,128]{2,1,0:T(8,128)S(1)} %pad_maximum_fusion.6), channel_id=1, replica_groups=mesh['gx'=8,'gy'=4] {'gy'}, dimensions={1}, use_global_device_ids=true | all-gather | bytes 81920 | tf_op jit(solution)/shard_map/all_gather | solution.py:52
  22.2 0.7 multiply_reduce_fusion.14
  22.9 1.4 pad_maximum_fusion.9
  24.3 40.2 %psum.28 = f32[2]{0:T(128)S(1)} all-reduce(f32[2]{0:T(128)S(1)} %pad_maximum_fusion.9), channel_id=1, replica_groups=mesh['gx'=8,'gy'=4] {'gx','gy'}, use_global_device_ids=true, to_apply=%region_2.4 | all-reduce | flops 2 | bytes 16 | tf_op jit(solution)/shard_map/psum | solution.py:70
  66.8 2.3 collective-permute-start.4
  69.1 2.5 %collective-permute-start.5 = (f32[16,1,128]{2,0,1:T(8,128)S(1)}, f32[16,1,128]{2,0,1:T(8,128)S(1)}, u32[]{:S(2)}, u32[]{:S(2)}) collective-permute-start(f32[16,1,128]{2,0,1:T(8,128)S(1)} %bitcast.113), channel_id=1, source_target_pairs={{4,0},{8,4},{12,8},{16,12},{20,16},{24,20},{28,24},{0,28},{5,1},{9... | collective-permute-start | bytes 24584 | tf_op jit(solution)/shard_map/ppermute | solution.py:17
  71.6 1.3 collective-permute-start.6
  72.9 3.0 %collective-permute-start.7 = (f32[1,16,128]{2,1,0:T(8,128)S(1)}, f32[1,16,128]{2,1,0:T(8,128)S(1)}, u32[]{:S(2)}, u32[]{:S(2)}) collective-permute-start(f32[1,16,128]{2,1,0:T(8,128)S(1)} %get-tuple-element.42), channel_id=1, source_target_pairs={{0,1},{1,2},{2,3},{4,5},{5,6},{6,7},{8,9},{9,10},{10,11},{12,13},{... | collective-permute-start | bytes 24584 | tf_op jit(solution)/shard_map/ppermute | solution.py:16
  75.9 5.8 %all_gather.10 = f32[2,64,128]{2,1,0:T(8,128)S(1)} all-gather(f32[2,16,128]{2,1,0:T(8,128)S(1)} %pad_maximum_fusion.7), channel_id=1, replica_groups=mesh['gx'=8,'gy'=4] {'gy'}, dimensions={1}, use_global_device_ids=true | all-gather | bytes 81920 | tf_op jit(solution)/shard_map/all_gather | solution.py:52
  83.1 0.8 multiply_reduce_fusion.8
  83.8 3.2 %stack.76 = f32[5]{0:T(128)S(1)} concatenate(f32[1]{0:T(128)} %bitcast.28, f32[1]{0:T(128)} %bitcast.29, f32[1]{0:T(128)} %bitcast.30, f32[1]{0:T(128)} %bitcast.31, f32[1]{0:T(128)} %bitcast.32), dimensions={0} | concatenate | bytes 40 | tf_op jit(solution)/shard_map/stack | solution.py:70
  87.1 37.9 %psum.29 = f32[5]{0:T(128)S(1)} all-reduce(f32[5]{0:T(128)S(1)} %stack.76), channel_id=1, replica_groups=mesh['gx'=8,'gy'=4] {'gx','gy'}, use_global_device_ids=true, to_apply=%region_8.10 | all-reduce | flops 5 | bytes 40 | tf_op jit(solution)/shard_map/psum | solution.py:70
  130.4 2.3 collective-permute-start.8
  132.7 2.5 %collective-permute-start.9 = (f32[16,1,128]{2,0,1:T(8,128)S(1)}, f32[16,1,128]{2,0,1:T(8,128)S(1)}, u32[]{:S(2)}, u32[]{:S(2)}) collective-permute-start(f32[16,1,128]{2,0,1:T(8,128)S(1)} %bitcast.114), channel_id=1, source_target_pairs={{4,0},{8,4},{12,8},{16,12},{20,16},{24,20},{28,24},{0,28},{5,1},{9... | collective-permute-start | bytes 24584 | tf_op jit(solution)/shard_map/ppermute | solution.py:17
  135.2 1.3 collective-permute-start.10
  136.5 3.0 %collective-permute-start.11 = (f32[1,16,128]{2,1,0:T(8,128)S(1)}, f32[1,16,128]{2,1,0:T(8,128)S(1)}, u32[]{:S(2)}, u32[]{:S(2)}) collective-permute-start(f32[1,16,128]{2,1,0:T(8,128)S(1)} %get-tuple-element.36), channel_id=1, source_target_pairs={{0,1},{1,2},{2,3},{4,5},{5,6},{6,7},{8,9},{9,10},{10,11},{12,13},{... | collective-permute-start | bytes 24584 | tf_op jit(solution)/shard_map/ppermute | solution.py:16
  139.6 5.8 %all_gather.11 = f32[2,64,128]{2,1,0:T(8,128)S(1)} all-gather(f32[2,16,128]{2,1,0:T(8,128)S(1)} %pad_maximum_fusion.8), channel_id=1, replica_groups=mesh['gx'=8,'gy'=4] {'gy'}, dimensions={1}, use_global_device_ids=true | all-gather | bytes 81920 | tf_op jit(solution)/shard_map/all_gather | solution.py:52
  146.7 0.9 multiply_reduce_fusion.1
  147.5 4.5 %stack.85 = f32[7]{0:T(128)S(1)} concatenate(f32[1]{0:T(128)} %bitcast.46, f32[1]{0:T(128)} %bitcast.47, f32[1]{0:T(128)} %bitcast.48, f32[1]{0:T(128)} %bitcast.49, f32[1]{0:T(128)} %bitcast.50, f32[1]{0:T(128)} %bitcast.51, f32[1]{0:T(128)} %bitcast.52), dimensions={0} | concatenate | bytes 56 | tf_op jit(solution)/shard_map/stack | solution.py:70
  152.0 38.1 %psum.30 = f32[7]{0:T(128)S(1)} all-reduce(f32[7]{0:T(128)S(1)} %stack.85), channel_id=1, replica_groups=mesh['gx'=8,'gy'=4] {'gx','gy'}, use_global_device_ids=true, to_apply=%region_16.18 | all-reduce | flops 7 | bytes 56 | tf_op jit(solution)/shard_map/psum | solution.py:70
  190.1 0.8 multiply_reduce_fusion.16
  194.1 2.6 %multiply_add_fusion = f32[16,16,128]{2,1,0:T(8,128)} fusion(f32[16,16,128]{2,1,0:T(8,128)S(1)} %fusion.27, f32[16,16,128]{2,1,0:T(8,128)S(1)} %fusion.29, f32[16,16,128]{2,1,0:T(8,128)S(1)} %convolution_bitcast_fusion, f32[]{:T(128)S(6)} %sqrt.17, f32[]{:T(128)} %bitcast.56, f32[]{:T(128)} %bitcast.55, f32[]{:T(128)S(6)} %mul.267, f32[]{:T(128)} %bitcast.34, ...), kind=kLoop, calls=%fused_computation.51 | loop fusion | flops 458752 | bytes 524324 | tf_op jit(solution)/shard_map/add | solution.py:84
  196.7 2.5 %multiply_reduce_fusion = (f32[]{:T(128)}, f32[16,16,128]{2,1,0:T(8,128)}) fusion(f32[16,16,128]{2,1,0:T(8,128)S(1)} %get-tuple-element.23, f32[]{:T(128)S(6)} %sqrt.17, f32[16,16,128]{2,1,0:T(8,128)S(1)} %get-tuple-element.24, f32[]{:T(128)} %bitcast.56, f32[16,16,128]{2,1,0:T(8,128)S(1)} %get-tuple-element.22, f32[16,16,128]{2,1,0:T(8,128)S(1)} %get-tuple-element.26, ...), kind=kLoop, calls=%fused_computation.49 | loop fusion | flops 327679 | bytes 655384 | tf_op jit(solution)/shard_map/reduce_sum | solution.py:23
  199.2 41.3 %psum.31 = f32[]{:T(128)} all-reduce(f32[]{:T(128)} %get-tuple-element.20), channel_id=1, replica_groups=mesh['gx'=8,'gy'=4] {'gx','gy'}, use_global_device_ids=true, to_apply=%region_20.22 | all-reduce | flops 1 | bytes 8 | tf_op jit(solution)/shard_map/psum | solution.py:88
  241.2 1.8 pad_maximum_fusion.10
  (64 shorter events, 8.5 us)
Async XLA Ops:
  0.6 0.9 copy-start
  2.7 18.8 %collective-permute-start.2 = (f32[1,16,128]{2,1,0:T(8,128)S(1)}, f32[1,16,128]{2,1,0:T(8,128)S(1)}, u32[]{:S(2)}, u32[]{:S(2)}) collective-permute-start(f32[1,16,128]{2,1,0:T(8,128)S(1)} %get-tuple-element.47), channel_id=1, source_target_pairs={{1,0},{2,1},{3,2},{5,4},{6,5},{7,6},{9,8},{10,9},{11,10},{13,12},{... | collective-permute-start | bytes 24584 | tf_op jit(solution)/shard_map/ppermute | solution.py:17
  4.0 17.5 %collective-permute-start.3 = (f32[1,16,128]{2,1,0:T(8,128)S(1)}, f32[1,16,128]{2,1,0:T(8,128)S(1)}, u32[]{:S(2)}, u32[]{:S(2)}) collective-permute-start(f32[1,16,128]{2,1,0:T(8,128)S(1)} %get-tuple-element.48), channel_id=1, source_target_pairs={{0,1},{1,2},{2,3},{4,5},{5,6},{6,7},{8,9},{9,10},{10,11},{12,13},{... | collective-permute-start | bytes 24584 | tf_op jit(solution)/shard_map/ppermute | solution.py:16
  7.1 7.7 %collective-permute-start = (f32[16,1,128]{2,0,1:T(8,128)S(1)}, f32[16,1,128]{2,0,1:T(8,128)S(1)}, u32[]{:S(2)}, u32[]{:S(2)}) collective-permute-start(f32[16,1,128]{2,0,1:T(8,128)S(1)} %bitcast.112), channel_id=1, source_target_pairs={{0,4},{4,8},{8,12},{12,16},{16,20},{20,24},{24,28},{28,0},{1,5},{5... | collective-permute-start | bytes 24584 | tf_op jit(solution)/shard_map/ppermute | solution.py:16
  10.1 4.7 %collective-permute-start.1 = (f32[16,1,128]{2,0,1:T(8,128)S(1)}, f32[16,1,128]{2,0,1:T(8,128)S(1)}, u32[]{:S(2)}, u32[]{:S(2)}) collective-permute-start(f32[16,1,128]{2,0,1:T(8,128)S(1)} %bitcast.111), channel_id=1, source_target_pairs={{4,0},{8,4},{12,8},{16,12},{20,16},{24,20},{28,24},{0,28},{5,1},{9... | collective-permute-start | bytes 24584 | tf_op jit(solution)/shard_map/ppermute | solution.py:17
  13.3 0.7 copy-start.5
  14.8 6.7 %copy-start.3 = (f32[16,16,128]{2,1,0:T(8,128)S(1)}, f32[16,16,128]{2,1,0:T(8,128)}, u32[]{:S(2)}) copy-start(f32[16,16,128]{2,1,0:T(8,128)} %param.9) | copy-start | bytes 393220
  20.2 1.3 copy-start.2
  20.2 1.3 copy-start.1
  21.5 0.7 copy-start.4
  66.8 9.1 %collective-permute-start.4 = (f32[16,1,128]{2,0,1:T(8,128)S(1)}, f32[16,1,128]{2,0,1:T(8,128)S(1)}, u32[]{:S(2)}, u32[]{:S(2)}) collective-permute-start(f32[16,1,128]{2,0,1:T(8,128)S(1)} %bitcast.115), channel_id=1, source_target_pairs={{0,4},{4,8},{8,12},{12,16},{16,20},{20,24},{24,28},{28,0},{1,5},{5... | collective-permute-start | bytes 24584 | tf_op jit(solution)/shard_map/ppermute | solution.py:16
  69.1 6.8 %collective-permute-start.5 = (f32[16,1,128]{2,0,1:T(8,128)S(1)}, f32[16,1,128]{2,0,1:T(8,128)S(1)}, u32[]{:S(2)}, u32[]{:S(2)}) collective-permute-start(f32[16,1,128]{2,0,1:T(8,128)S(1)} %bitcast.113), channel_id=1, source_target_pairs={{4,0},{8,4},{12,8},{16,12},{20,16},{24,20},{28,24},{0,28},{5,1},{9... | collective-permute-start | bytes 24584 | tf_op jit(solution)/shard_map/ppermute | solution.py:17
  71.6 11.5 %collective-permute-start.6 = (f32[1,16,128]{2,1,0:T(8,128)S(1)}, f32[1,16,128]{2,1,0:T(8,128)S(1)}, u32[]{:S(2)}, u32[]{:S(2)}) collective-permute-start(f32[1,16,128]{2,1,0:T(8,128)S(1)} %get-tuple-element.41), channel_id=1, source_target_pairs={{1,0},{2,1},{3,2},{5,4},{6,5},{7,6},{9,8},{10,9},{11,10},{13,12},{... | collective-permute-start | bytes 24584 | tf_op jit(solution)/shard_map/ppermute | solution.py:17
  72.9 10.2 %collective-permute-start.7 = (f32[1,16,128]{2,1,0:T(8,128)S(1)}, f32[1,16,128]{2,1,0:T(8,128)S(1)}, u32[]{:S(2)}, u32[]{:S(2)}) collective-permute-start(f32[1,16,128]{2,1,0:T(8,128)S(1)} %get-tuple-element.42), channel_id=1, source_target_pairs={{0,1},{1,2},{2,3},{4,5},{5,6},{6,7},{8,9},{9,10},{10,11},{12,13},{... | collective-permute-start | bytes 24584 | tf_op jit(solution)/shard_map/ppermute | solution.py:16
  130.4 9.1 %collective-permute-start.8 = (f32[16,1,128]{2,0,1:T(8,128)S(1)}, f32[16,1,128]{2,0,1:T(8,128)S(1)}, u32[]{:S(2)}, u32[]{:S(2)}) collective-permute-start(f32[16,1,128]{2,0,1:T(8,128)S(1)} %bitcast.116), channel_id=1, source_target_pairs={{0,4},{4,8},{8,12},{12,16},{16,20},{20,24},{24,28},{28,0},{1,5},{5... | collective-permute-start | bytes 24584 | tf_op jit(solution)/shard_map/ppermute | solution.py:16
  132.7 6.8 %collective-permute-start.9 = (f32[16,1,128]{2,0,1:T(8,128)S(1)}, f32[16,1,128]{2,0,1:T(8,128)S(1)}, u32[]{:S(2)}, u32[]{:S(2)}) collective-permute-start(f32[16,1,128]{2,0,1:T(8,128)S(1)} %bitcast.114), channel_id=1, source_target_pairs={{4,0},{8,4},{12,8},{16,12},{20,16},{24,20},{28,24},{0,28},{5,1},{9... | collective-permute-start | bytes 24584 | tf_op jit(solution)/shard_map/ppermute | solution.py:17
  135.2 11.5 %collective-permute-start.10 = (f32[1,16,128]{2,1,0:T(8,128)S(1)}, f32[1,16,128]{2,1,0:T(8,128)S(1)}, u32[]{:S(2)}, u32[]{:S(2)}) collective-permute-start(f32[1,16,128]{2,1,0:T(8,128)S(1)} %get-tuple-element.35), channel_id=1, source_target_pairs={{1,0},{2,1},{3,2},{5,4},{6,5},{7,6},{9,8},{10,9},{11,10},{13,12},{... | collective-permute-start | bytes 24584 | tf_op jit(solution)/shard_map/ppermute | solution.py:17
  136.5 10.2 %collective-permute-start.11 = (f32[1,16,128]{2,1,0:T(8,128)S(1)}, f32[1,16,128]{2,1,0:T(8,128)S(1)}, u32[]{:S(2)}, u32[]{:S(2)}) collective-permute-start(f32[1,16,128]{2,1,0:T(8,128)S(1)} %get-tuple-element.36), channel_id=1, source_target_pairs={{0,1},{1,2},{2,3},{4,5},{5,6},{6,7},{8,9},{9,10},{10,11},{12,13},{... | collective-permute-start | bytes 24584 | tf_op jit(solution)/shard_map/ppermute | solution.py:16
where the time goes:
time: 244 us; the launch traced here: 243 us
  blocking collectives  175 us (72%)
  starting transfers between devices  28.6 us (12%)
  local copies, waits for them, and re-layouts  15.2 us (6%)
  other arithmetic  12.7 us (5%)
  between operations  9.45 us (4%)
    psum x3, blocking collectives, on_device(): totals = lax.psum(jnp.stack(terms), ('gx', 'gy')) / total_cells  116 us
    psum x1, blocking collectives, on_device(): lax.psum(local_product(residual, residual), ('gx', 'gy')) / total_cells  41.3 us
    all_gather x3, blocking collectives, on_device(): whole = lax.all_gather(edges, 'gy', axis=1, tiled=True)  17 us
    ppermute x6, starting transfers between devices, padded(): before = lax.ppermute(last, axis, up)  16.8 us
    ppermute x6, starting transfers between devices, padded(): after = lax.ppermute(initial, axis, down)  11.9 us
    another operation x2, local copies, waits for them, and re-layouts, on_device(): totals = lax.psum(jnp.stack(terms), ('gx', 'gy')) / total_cells  7.69 us
    reduce_sum x4, other arithmetic, local_product(): return jnp.sum(left * right)  4.94 us
  transfers between devices with their start and end apart: 12, of which 1 were waited for; matrix products, arithmetic and copies ran while one was open for 2% of the time, Pallas kernels for 0%

commit v1 on v0

--- a/solution.py
+++ b/solution.py
@@ -67,7 +67,7 @@
         terms = terms + [local_product(image, image), local_product(residual, image)]
         if step > 0:
             terms.append(local_product(residual, residual))
-        totals = lax.psum(jnp.stack(terms), ("gx", "gy")) / total_cells
+        totals = jnp.sum(lax.all_gather(jnp.stack(terms), ("gx", "gy")), axis=0) / total_cells
         coeffs = totals[:count]
         against = totals[count : 2 * count]
         square = totals[2 * count] - jnp.sum(coeffs * coeffs)

time: 244 us -> 242 us (level)
  blocking collectives: 175 us -> 172 us
    psum x3 -> x0, blocking collectives: 116 us -> none  [on_device(): totals = lax.psum(jnp.stack(terms), ('gx', 'gy')) / total_cells]
    unnamed x0 -> x3, blocking collectives: none -> 114 us
  transfers between devices with their start and end apart: 12 -> 12, of which waited for: 1 -> 0; matrix products, arithmetic and copies ran while one was open for 2% -> 2% of each run, Pallas kernels for 0% -> 0%
where the time goes in v1:
time: 242 us; the launch traced here: 241 us
  blocking collectives  172 us (71%)
  starting transfers between devices  28.6 us (12%)
  local copies, waits for them, and re-layouts  15.9 us (7%)
  other arithmetic  12.9 us (5%)
  between operations  9.51 us (4%)
    unnamed x3, blocking collectives  114 us
    psum x1, blocking collectives, on_device(): lax.psum(local_product(residual, residual), ('gx', 'gy')) / total_cells  41.5 us
    all_gather x3, blocking collectives, on_device(): whole = lax.all_gather(edges, 'gy', axis=1, tiled=True)  17 us
    ppermute x6, starting transfers between devices, padded(): before = lax.ppermute(last, axis, up)  16.8 us
    ppermute x6, starting transfers between devices, padded(): after = lax.ppermute(initial, axis, down)  11.9 us
    another operation x2, local copies, waits for them, and re-layouts, on_device(): jnp.stack(terms)  7.69 us
    reduce_sum x4, other arithmetic, local_product(): return jnp.sum(left * right)  4.94 us
  transfers between devices with their start and end apart: 12, of which 0 were waited for; matrix products, arithmetic and copies ran while one was open for 2% of the time, Pallas kernels for 0%

profile of v1, /device:TPU:0, one launch (start us, length us, event | category | flops | bytes accessed | tf_op | source)
XLA Modules:
  0.0 241.1 jit_solution(4157309998689740637)
XLA Ops:
  0.7 0.9 copy-done
  1.5 1.2 convolution_bitcast_fusion
  2.7 3.0 %collective-permute-start = (f32[16,1,128]{2,0,1:T(8,128)S(1)}, f32[16,1,128]{2,0,1:T(8,128)S(1)}, u32[]{:S(2)}, u32[]{:S(2)}) collective-permute-start(f32[16,1,128]{2,0,1:T(8,128)S(1)} %bitcast.112), channel_id=1, source_target_pairs={{0,4},{4,8},{8,12},{12,16},{16,20},{20,24},{24,28},{28,0},{1,5},{5... | collective-permute-start | bytes 24584 | tf_op jit(solution)/shard_map/ppermute | solution.py:16
  5.8 3.1 %collective-permute-start.1 = (f32[16,1,128]{2,0,1:T(8,128)S(1)}, f32[16,1,128]{2,0,1:T(8,128)S(1)}, u32[]{:S(2)}, u32[]{:S(2)}) collective-permute-start(f32[16,1,128]{2,0,1:T(8,128)S(1)} %bitcast.111), channel_id=1, source_target_pairs={{4,0},{8,4},{12,8},{16,12},{20,16},{24,20},{28,24},{0,28},{5,1},{9... | collective-permute-start | bytes 24584 | tf_op jit(solution)/shard_map/ppermute | solution.py:17
  8.9 1.3 collective-permute-start.2
  10.2 3.0 %collective-permute-start.3 = (f32[1,16,128]{2,1,0:T(8,128)S(1)}, f32[1,16,128]{2,1,0:T(8,128)S(1)}, u32[]{:S(2)}, u32[]{:S(2)}) collective-permute-start(f32[1,16,128]{2,1,0:T(8,128)S(1)} %get-tuple-element.48), channel_id=1, source_target_pairs={{0,1},{1,2},{2,3},{4,5},{5,6},{6,7},{8,9},{9,10},{10,11},{12,13},{... | collective-permute-start | bytes 24584 | tf_op jit(solution)/shard_map/ppermute | solution.py:16
  13.3 0.7 copy-done.5
  14.2 5.4 %all_gather.27 = f32[2,64,128]{2,1,0:T(8,128)S(1)} all-gather(f32[2,16,128]{2,1,0:T(8,128)S(1)} %pad_maximum_fusion.6), channel_id=1, replica_groups=mesh['gx'=8,'gy'=4] {'gy'}, dimensions={1}, use_global_device_ids=true | all-gather | bytes 81920 | tf_op jit(solution)/shard_map/all_gather | solution.py:52
  21.6 0.7 multiply_reduce_fusion.14
  22.3 1.5 maximum_dynamic-update-slice_fusion
  23.8 37.8 %all-reduce.3 = f32[64]{0:T(128)S(1)} all-reduce(f32[64]{0:T(128)S(1)} %maximum_dynamic-update-slice_fusion), channel_id=2, replica_groups=mesh['gx'=8,'gy'=4] {'gx','gy'}, use_global_device_ids=true, to_apply=%add.3 | all-reduce | flops 64 | bytes 512
  64.0 2.3 collective-permute-start.4
  66.3 2.5 %collective-permute-start.5 = (f32[16,1,128]{2,0,1:T(8,128)S(1)}, f32[16,1,128]{2,0,1:T(8,128)S(1)}, u32[]{:S(2)}, u32[]{:S(2)}) collective-permute-start(f32[16,1,128]{2,0,1:T(8,128)S(1)} %bitcast.113), channel_id=1, source_target_pairs={{4,0},{8,4},{12,8},{16,12},{20,16},{24,20},{28,24},{0,28},{5,1},{9... | collective-permute-start | bytes 24584 | tf_op jit(solution)/shard_map/ppermute | solution.py:17
  68.8 1.3 collective-permute-start.6
  70.1 3.0 %collective-permute-start.7 = (f32[1,16,128]{2,1,0:T(8,128)S(1)}, f32[1,16,128]{2,1,0:T(8,128)S(1)}, u32[]{:S(2)}, u32[]{:S(2)}) collective-permute-start(f32[1,16,128]{2,1,0:T(8,128)S(1)} %get-tuple-element.42), channel_id=1, source_target_pairs={{0,1},{1,2},{2,3},{4,5},{5,6},{6,7},{8,9},{9,10},{10,11},{12,13},{... | collective-permute-start | bytes 24584 | tf_op jit(solution)/shard_map/ppermute | solution.py:16
  73.2 5.8 %all_gather.30 = f32[2,64,128]{2,1,0:T(8,128)S(1)} all-gather(f32[2,16,128]{2,1,0:T(8,128)S(1)} %pad_maximum_fusion.7), channel_id=1, replica_groups=mesh['gx'=8,'gy'=4] {'gy'}, dimensions={1}, use_global_device_ids=true | all-gather | bytes 81920 | tf_op jit(solution)/shard_map/all_gather | solution.py:52
  80.3 0.8 multiply_reduce_fusion.8
  81.1 3.2 %stack.76 = f32[5]{0:T(128)S(1)} concatenate(f32[1]{0:T(128)} %bitcast.28, f32[1]{0:T(128)} %bitcast.29, f32[1]{0:T(128)} %bitcast.30, f32[1]{0:T(128)} %bitcast.31, f32[1]{0:T(128)} %bitcast.32), dimensions={0} | concatenate | bytes 40 | tf_op jit(solution)/shard_map/stack | solution.py:70
  84.5 38.0 %all-reduce.4 = f32[160]{0:T(256)S(1)} all-reduce(f32[160]{0:T(256)S(1)} %dynamic-update-slice.1), channel_id=3, replica_groups=mesh['gx'=8,'gy'=4] {'gx','gy'}, use_global_device_ids=true, to_apply=%add.4 | all-reduce | flops 160 | bytes 1280
  128.1 2.3 collective-permute-start.8
  130.4 2.5 %collective-permute-start.9 = (f32[16,1,128]{2,0,1:T(8,128)S(1)}, f32[16,1,128]{2,0,1:T(8,128)S(1)}, u32[]{:S(2)}, u32[]{:S(2)}) collective-permute-start(f32[16,1,128]{2,0,1:T(8,128)S(1)} %bitcast.114), channel_id=1, source_target_pairs={{4,0},{8,4},{12,8},{16,12},{20,16},{24,20},{28,24},{0,28},{5,1},{9... | collective-permute-start | bytes 24584 | tf_op jit(solution)/shard_map/ppermute | solution.py:17
  132.9 1.3 collective-permute-start.10
  134.2 3.0 %collective-permute-start.11 = (f32[1,16,128]{2,1,0:T(8,128)S(1)}, f32[1,16,128]{2,1,0:T(8,128)S(1)}, u32[]{:S(2)}, u32[]{:S(2)}) collective-permute-start(f32[1,16,128]{2,1,0:T(8,128)S(1)} %get-tuple-element.36), channel_id=1, source_target_pairs={{0,1},{1,2},{2,3},{4,5},{5,6},{6,7},{8,9},{9,10},{10,11},{12,13},{... | collective-permute-start | bytes 24584 | tf_op jit(solution)/shard_map/ppermute | solution.py:16
  137.3 5.8 %all_gather.33 = f32[2,64,128]{2,1,0:T(8,128)S(1)} all-gather(f32[2,16,128]{2,1,0:T(8,128)S(1)} %pad_maximum_fusion.8), channel_id=1, replica_groups=mesh['gx'=8,'gy'=4] {'gy'}, dimensions={1}, use_global_device_ids=true | all-gather | bytes 81920 | tf_op jit(solution)/shard_map/all_gather | solution.py:52
  144.4 0.9 multiply_reduce_fusion.1
  145.2 4.5 %stack.85 = f32[7]{0:T(128)S(1)} concatenate(f32[1]{0:T(128)} %bitcast.46, f32[1]{0:T(128)} %bitcast.47, f32[1]{0:T(128)} %bitcast.48, f32[1]{0:T(128)} %bitcast.49, f32[1]{0:T(128)} %bitcast.50, f32[1]{0:T(128)} %bitcast.51, f32[1]{0:T(128)} %bitcast.52), dimensions={0} | concatenate | bytes 56 | tf_op jit(solution)/shard_map/stack | solution.py:70
  149.9 38.0 %all-reduce.5 = f32[224]{0:T(256)S(1)} all-reduce(f32[224]{0:T(256)S(1)} %dynamic-update-slice.2), channel_id=4, replica_groups=mesh['gx'=8,'gy'=4] {'gx','gy'}, use_global_device_ids=true, to_apply=%add.5 | all-reduce | flops 224 | bytes 1792
  188.7 0.8 multiply_reduce_fusion.16
  192.1 2.6 %multiply_add_fusion = f32[16,16,128]{2,1,0:T(8,128)} fusion(f32[16,16,128]{2,1,0:T(8,128)S(1)} %fusion.27, f32[16,16,128]{2,1,0:T(8,128)S(1)} %fusion.29, f32[16,16,128]{2,1,0:T(8,128)S(1)} %convolution_bitcast_fusion, f32[]{:T(128)S(6)} %sqrt.17, f32[]{:T(128)} %bitcast.56, f32[]{:T(128)} %bitcast.55, f32[]{:T(128)S(6)} %mul.267, f32[]{:T(128)} %bitcast.34, ...), kind=kLoop, calls=%fused_computation.51 | loop fusion | flops 458752 | bytes 524324 | tf_op jit(solution)/shard_map/add | solution.py:84
  194.6 2.5 %multiply_reduce_fusion = (f32[]{:T(128)}, f32[16,16,128]{2,1,0:T(8,128)}) fusion(f32[16,16,128]{2,1,0:T(8,128)S(1)} %get-tuple-element.23, f32[]{:T(128)S(6)} %sqrt.17, f32[16,16,128]{2,1,0:T(8,128)S(1)} %get-tuple-element.24, f32[]{:T(128)} %bitcast.56, f32[16,16,128]{2,1,0:T(8,128)S(1)} %get-tuple-element.22, f32[16,16,128]{2,1,0:T(8,128)S(1)} %get-tuple-element.26, ...), kind=kLoop, calls=%fused_computation.49 | loop fusion | flops 327679 | bytes 655384 | tf_op jit(solution)/shard_map/reduce_sum | solution.py:23
  197.2 41.5 %psum.7 = f32[]{:T(128)} all-reduce(f32[]{:T(128)} %get-tuple-element.20), channel_id=1, replica_groups=mesh['gx'=8,'gy'=4] {'gx','gy'}, use_global_device_ids=true, to_apply=%region_20.22 | all-reduce | flops 1 | bytes 8 | tf_op jit(solution)/shard_map/psum | solution.py:88
  239.3 1.8 pad_maximum_fusion.9
  (75 shorter events, 8.7 us)
Async XLA Ops:
  0.6 0.9 copy-start
  2.7 11.4 %collective-permute-start = (f32[16,1,128]{2,0,1:T(8,128)S(1)}, f32[16,1,128]{2,0,1:T(8,128)S(1)}, u32[]{:S(2)}, u32[]{:S(2)}) collective-permute-start(f32[16,1,128]{2,0,1:T(8,128)S(1)} %bitcast.112), channel_id=1, source_target_pairs={{0,4},{4,8},{8,12},{12,16},{16,20},{20,24},{24,28},{28,0},{1,5},{5... | collective-permute-start | bytes 24584 | tf_op jit(solution)/shard_map/ppermute | solution.py:16
  5.8 8.4 %collective-permute-start.1 = (f32[16,1,128]{2,0,1:T(8,128)S(1)}, f32[16,1,128]{2,0,1:T(8,128)S(1)}, u32[]{:S(2)}, u32[]{:S(2)}) collective-permute-start(f32[16,1,128]{2,0,1:T(8,128)S(1)} %bitcast.111), channel_id=1, source_target_pairs={{4,0},{8,4},{12,8},{16,12},{20,16},{24,20},{28,24},{0,28},{5,1},{9... | collective-permute-start | bytes 24584 | tf_op jit(solution)/shard_map/ppermute | solution.py:17
  8.9 12.0 %collective-permute-start.2 = (f32[1,16,128]{2,1,0:T(8,128)S(1)}, f32[1,16,128]{2,1,0:T(8,128)S(1)}, u32[]{:S(2)}, u32[]{:S(2)}) collective-permute-start(f32[1,16,128]{2,1,0:T(8,128)S(1)} %get-tuple-element.47), channel_id=1, source_target_pairs={{1,0},{2,1},{3,2},{5,4},{6,5},{7,6},{9,8},{10,9},{11,10},{13,12},{... | collective-permute-start | bytes 24584 | tf_op jit(solution)/shard_map/ppermute | solution.py:17
  10.2 10.7 %collective-permute-start.3 = (f32[1,16,128]{2,1,0:T(8,128)S(1)}, f32[1,16,128]{2,1,0:T(8,128)S(1)}, u32[]{:S(2)}, u32[]{:S(2)}) collective-permute-start(f32[1,16,128]{2,1,0:T(8,128)S(1)} %get-tuple-element.48), channel_id=1, source_target_pairs={{0,1},{1,2},{2,3},{4,5},{5,6},{6,7},{8,9},{9,10},{10,11},{12,13},{... | collective-permute-start | bytes 24584 | tf_op jit(solution)/shard_map/ppermute | solution.py:16
  13.3 0.7 copy-start.5
  14.2 6.7 %copy-start.3 = (f32[16,16,128]{2,1,0:T(8,128)S(1)}, f32[16,16,128]{2,1,0:T(8,128)}, u32[]{:S(2)}) copy-start(f32[16,16,128]{2,1,0:T(8,128)} %param.9) | copy-start | bytes 393220
  19.6 1.3 copy-start.2
  19.6 1.3 copy-start.1
  20.9 0.7 copy-start.4
  64.0 9.1 %collective-permute-start.4 = (f32[16,1,128]{2,0,1:T(8,128)S(1)}, f32[16,1,128]{2,0,1:T(8,128)S(1)}, u32[]{:S(2)}, u32[]{:S(2)}) collective-permute-start(f32[16,1,128]{2,0,1:T(8,128)S(1)} %bitcast.115), channel_id=1, source_target_pairs={{0,4},{4,8},{8,12},{12,16},{16,20},{20,24},{24,28},{28,0},{1,5},{5... | collective-permute-start | bytes 24584 | tf_op jit(solution)/shard_map/ppermute | solution.py:16
  66.3 6.8 %collective-permute-start.5 = (f32[16,1,128]{2,0,1:T(8,128)S(1)}, f32[16,1,128]{2,0,1:T(8,128)S(1)}, u32[]{:S(2)}, u32[]{:S(2)}) collective-permute-start(f32[16,1,128]{2,0,1:T(8,128)S(1)} %bitcast.113), channel_id=1, source_target_pairs={{4,0},{8,4},{12,8},{16,12},{20,16},{24,20},{28,24},{0,28},{5,1},{9... | collective-permute-start | bytes 24584 | tf_op jit(solution)/shard_map/ppermute | solution.py:17
  68.8 11.5 %collective-permute-start.6 = (f32[1,16,128]{2,1,0:T(8,128)S(1)}, f32[1,16,128]{2,1,0:T(8,128)S(1)}, u32[]{:S(2)}, u32[]{:S(2)}) collective-permute-start(f32[1,16,128]{2,1,0:T(8,128)S(1)} %get-tuple-element.41), channel_id=1, source_target_pairs={{1,0},{2,1},{3,2},{5,4},{6,5},{7,6},{9,8},{10,9},{11,10},{13,12},{... | collective-permute-start | bytes 24584 | tf_op jit(solution)/shard_map/ppermute | solution.py:17
  70.1 10.2 %collective-permute-start.7 = (f32[1,16,128]{2,1,0:T(8,128)S(1)}, f32[1,16,128]{2,1,0:T(8,128)S(1)}, u32[]{:S(2)}, u32[]{:S(2)}) collective-permute-start(f32[1,16,128]{2,1,0:T(8,128)S(1)} %get-tuple-element.42), channel_id=1, source_target_pairs={{0,1},{1,2},{2,3},{4,5},{5,6},{6,7},{8,9},{9,10},{10,11},{12,13},{... | collective-permute-start | bytes 24584 | tf_op jit(solution)/shard_map/ppermute | solution.py:16
  128.1 9.1 %collective-permute-start.8 = (f32[16,1,128]{2,0,1:T(8,128)S(1)}, f32[16,1,128]{2,0,1:T(8,128)S(1)}, u32[]{:S(2)}, u32[]{:S(2)}) collective-permute-start(f32[16,1,128]{2,0,1:T(8,128)S(1)} %bitcast.116), channel_id=1, source_target_pairs={{0,4},{4,8},{8,12},{12,16},{16,20},{20,24},{24,28},{28,0},{1,5},{5... | collective-permute-start | bytes 24584 | tf_op jit(solution)/shard_map/ppermute | solution.py:16
  130.4 6.8 %collective-permute-start.9 = (f32[16,1,128]{2,0,1:T(8,128)S(1)}, f32[16,1,128]{2,0,1:T(8,128)S(1)}, u32[]{:S(2)}, u32[]{:S(2)}) collective-permute-start(f32[16,1,128]{2,0,1:T(8,128)S(1)} %bitcast.114), channel_id=1, source_target_pairs={{4,0},{8,4},{12,8},{16,12},{20,16},{24,20},{28,24},{0,28},{5,1},{9... | collective-permute-start | bytes 24584 | tf_op jit(solution)/shard_map/ppermute | solution.py:17
  132.9 11.5 %collective-permute-start.10 = (f32[1,16,128]{2,1,0:T(8,128)S(1)}, f32[1,16,128]{2,1,0:T(8,128)S(1)}, u32[]{:S(2)}, u32[]{:S(2)}) collective-permute-start(f32[1,16,128]{2,1,0:T(8,128)S(1)} %get-tuple-element.35), channel_id=1, source_target_pairs={{1,0},{2,1},{3,2},{5,4},{6,5},{7,6},{9,8},{10,9},{11,10},{13,12},{... | collective-permute-start | bytes 24584 | tf_op jit(solution)/shard_map/ppermute | solution.py:17
  134.2 10.2 %collective-permute-start.11 = (f32[1,16,128]{2,1,0:T(8,128)S(1)}, f32[1,16,128]{2,1,0:T(8,128)S(1)}, u32[]{:S(2)}, u32[]{:S(2)}) collective-permute-start(f32[1,16,128]{2,1,0:T(8,128)S(1)} %get-tuple-element.36), channel_id=1, source_target_pairs={{0,1},{1,2},{2,3},{4,5},{5,6},{6,7},{8,9},{9,10},{10,11},{12,13},{... | collective-permute-start | bytes 24584 | tf_op jit(solution)/shard_map/ppermute | solution.py:16
